TPU v7x, 32 devices: a whole 2x2x4 slice. The times are simulated.
32 devices in a mesh: grp: 4 (over y, core), dev: 8 (over z, x).
Axes of the slice: x: 2, y: 2, z: 4, core: 2. Of those that a mesh axis runs over, the one named last changes fastest.
Arguments:
- spectra: bfloat16 [96, 2, 16384], P(('grp', 'dev')), may hold values from -6 to 6
- partners: int32 [32, 8], P(('grp', 'dev')), may hold values from 0 to 7, all different within a row
- owners: int32 [256, 1], P(('grp', 'dev')), may hold values from 0 to 3; in each aligned block of 8 rows (0 to 7, 8 to 15, ...) at most 2 rows name the same one
- counts: int32 [4], replicated, may hold values from 12 to 24, as said below
- gain: float32 [8192], replicated, may hold values from 0.05 to 1
Outputs:
- coherence: bfloat16 [256, 3, 3, 16384], P(('grp', 'dev'))
Inputs may be any that keep to these rules, and one draw needn't show every extreme that they name: `partners`: the 8 entries of a row are distinct. `owners`: of the 8 slots of one device, at most 2 have the same owner group, and exactly 2 do for some device. `counts`: some group has all 24 stations live and some has half of them.
All inputs are finite; a program needn't handle non-finite values.
Results may differ from a plain program's by a relative error of at most 0.0054.
Values may be sent and summed in bfloat16 or wider, within the bound.
A program may use at most 64 MiB of HBM per device.

v0:
```python
import jax
import jax.numpy as jnp
from jax import lax
from jax.sharding import PartitionSpec as P

CAP = 2


EPS = 1e-06


def cross_spectra(own, part):
    half = own.shape[-1] // 2
    own_f = own.astype(jnp.float32)
    part_f = part.astype(jnp.float32)
    a_own = own_f[..., :, None, :, :half]
    b_own = own_f[..., :, None, :, half:]
    a_part = part_f[..., None, :, :, :half]
    b_part = part_f[..., None, :, :, half:]
    real_part = jnp.sum(a_own * a_part + b_own * b_part, axis=-2)
    imag_part = jnp.sum(b_own * a_part - a_own * b_part, axis=-2)
    return jnp.concatenate([real_part, imag_part], axis=-1)


def energies(block, gain_two):
    values = block.astype(jnp.float32)
    total = jnp.sum(gain_two * values * values, axis=(-2, -1))
    return total / (values.shape[-2] * values.shape[-1])


def normalize(stack, e_own, e_part, windows):
    e_own = e_own.astype(jnp.float32)
    e_part = e_part.astype(jnp.float32)
    denom = windows * jnp.sqrt((e_own[..., :, None] + EPS) * (e_part[..., None, :] + EPS))
    return (stack.astype(jnp.float32) / denom[..., None]).astype(jnp.bfloat16)


def body(spectra, partners, owners, counts, gain):
    groups = lax.axis_size("grp")
    group = lax.axis_index("grp")
    device = lax.axis_index("dev")
    per_dev = spectra.shape[0]
    windows = spectra.shape[1]
    gain_two = jnp.concatenate([gain, gain])
    group_count = jnp.sum(jnp.where(jnp.arange(groups) == group, counts, 0))
    station = device * per_dev + jnp.arange(per_dev, dtype=jnp.int32)
    live = (station < group_count).astype(jnp.bfloat16)
    masked = spectra * live[:, None, None]
    blocks = partners[0]
    slots = blocks.shape[0]
    wanted = blocks[:, None] * per_dev + jnp.arange(per_dev, dtype=jnp.int32)[None, :]
    piece = lax.all_gather(masked, "dev", axis=0, tiled=True)
    rows = jnp.arange(piece.shape[0], dtype=jnp.int32)
    select = (wanted[:, :, None] == rows[None, None, :]).astype(jnp.bfloat16)
    taken = jnp.einsum("psr,rwf->pswf", select, piece, preferred_element_type=jnp.float32)
    partner_spec = taken.astype(jnp.bfloat16)
    owner = owners[:, 0]
    slot = jnp.arange(slots, dtype=jnp.int32)
    earlier = slot[None, :] < slot[:, None]
    same = owner[:, None] == owner[None, :]
    rank = jnp.sum((same & earlier).astype(jnp.int32), axis=1)
    dest = owner * CAP + rank
    place = (jnp.arange(groups * CAP, dtype=jnp.int32)[:, None] == dest[None, :]).astype(
        jnp.bfloat16
    )
    own_all = jnp.broadcast_to(masked, partner_spec.shape)
    stack = (cross_spectra(own_all, partner_spec) * gain_two).astype(jnp.bfloat16)
    energy_pair = jnp.stack(
        [energies(own_all, gain_two), energies(partner_spec, gain_two)], axis=1
    ).astype(jnp.bfloat16)
    send_stack = jnp.einsum(
        "kp,pijf->kijf", place, stack, preferred_element_type=jnp.float32
    ).astype(jnp.bfloat16)
    send_energy = jnp.einsum(
        "kp,pcs->kcs", place, energy_pair, preferred_element_type=jnp.float32
    ).astype(jnp.bfloat16)
    send_stack = send_stack.reshape((groups, CAP) + send_stack.shape[1:])
    send_energy = send_energy.reshape((groups, CAP) + send_energy.shape[1:])
    stacks_in = lax.all_to_all(send_stack, "grp", split_axis=0, concat_axis=0, tiled=True)
    energy_in = lax.all_to_all(send_energy, "grp", split_axis=0, concat_axis=0, tiled=True)
    result = normalize(stacks_in, energy_in[:, :, 0], energy_in[:, :, 1], windows)
    return result.reshape((groups * CAP,) + result.shape[2:])


def solution(mesh):
    in_specs = (
        P(("grp", "dev"), None, None),
        P(("grp", "dev"), None),
        P(("grp", "dev"), None),
        P(),
        P(),
    )
    out_specs = P(("grp", "dev"), None, None, None)
    return jax.shard_map(body, mesh=mesh, in_specs=in_specs, out_specs=out_specs, check_vma=False)
```

profile of v0, /device:TPU:0, one launch (start us, length us, event | category | flops | bytes accessed | tf_op | source)
XLA Modules:
  0.0 122.6 jit_solution(163293112452649837)
XLA Ops:
  6.5 0.0 all-gather.2.cloned.1.call-start
  6.5 1.3 %fusion.23 = s32[]{:T(128)} fusion(s32[4]{0:T(128)} %param.8, s32[]{:T(128)S(6)} %axis_index.25), kind=kLoop, calls=%fused_computation.43 | loop fusion | flops 11 | bytes 24 | tf_op jit(solution)/shard_map/reduce_sum | solution.py:45
  7.8 0.6 compare_convert_fusion
  8.5 1.9 %fusion.26 = (f32[3,2,16384]{2,1,0:T(2,128)S(1)}, bf16[3,2,16384]{2,1,0:T(2,128)(2,1)}) fusion(bf16[3,2,16384]{2,1,0:T(2,128)(2,1)} %param.5, bf16[3]{0:T(256)(128)(2,1)S(1)} %compare_convert_fusion), kind=kLoop, calls=%fused_computation.48 | loop fusion | flops 196608 | bytes 786438 | tf_op jit(solution)/shard_map/convert_element_type | solution.py:14
  10.4 0.0 all-gather.2.cloned.1.call-update
  10.4 0.8 constant_dynamic-update-slice_fusion.1
  11.2 0.8 constant_dynamic-update-slice_fusion
  11.9 0.9 convert_reduce_fusion
  12.8 0.7 multiply_bitcast_fusion
  13.5 0.7 multiply_add_fusion
  14.2 1.1 fusion.28
  15.2 42.2 %all-gather.2.cloned.1.call-done = bf16[24,2,16384]{2,1,0:T(2,128)(2,1)} async-done(((bf16[3,2,16384]{2,1,0:T(2,128)(2,1)}), bf16[24,2,16384]{2,1,0:T(2,128)(2,1)}) %all-gather.2.cloned.1.call-update) | async-done | bytes 1572880 | tf_op jit(solution)/shard_map/all_gather | solution.py:52
  57.4 4.0 %multiply_reduce_fusion = (f32[8,3]{0,1:T(4,128)S(1)}, f32[8,3]{0,1:T(4,128)S(1)}, f32[8,3,2,16384]{3,0,2,1:T(8,128)S(1)}) fusion(f32[3,2,16384]{2,1,0:T(2,128)S(1)} %get-tuple-element.9, f32[16384]{0:T(1024)S(1)} %constant_dynamic-update-slice_fusion, bf16[24,2,16384]{2,1,0:T(2,128)(2,1)} %all-gather.2.cloned.1.call-done, s32[8,3]{0,1:T(4,128)S(1)} %iota_add_fusion), kind=kOutput, calls=%fused_computation.11 | convolution fusion | flops 44040720 | bytes 5177632 | tf_op jit(solution)/shard_map/psr,rwf->pswf/dot_general | solution.py:55
  61.4 0.2 fusion.27
  61.6 1.4 %add_reduce_fusion = (f32[8,3,3,8192]{3,0,2,1:T(8,128)S(1)}, f32[8,3,3,8192]{3,0,2,1:T(8,128)S(1)}) fusion(f32[8,3,2,8192]{3,0,2,1:T(8,128)S(1)} %get-tuple-element.12, f32[3,2,8192]{2,1,0:T(2,128)S(1)} %get-tuple-element.14, f32[8,3,2,8192]{3,0,2,1:T(8,128)S(1)} %get-tuple-element.11, f32[3,2,8192]{2,1,0:T(2,128)S(1)} %get-tuple-element.13), kind=kLoop, calls=%fused_computation.9 | loop fusion | flops 8257536 | bytes 8257536 | tf_op jit(solution)/shard_map/reduce_sum | solution.py:20
  63.1 0.8 convolution_convert_fusion
  63.8 2.8 %reshape.90 = bf16[4,2,3,3,16384]{4,1,0,3,2:T(2,128)(2,1)} reshape(bf16[8,3,3,16384]{3,0,2,1:T(8,128)(2,1)S(1)} %convolution_convert_fusion) | data formatting | bytes 4718592 | tf_op jit(solution)/shard_map/reshape | solution.py:77
  66.6 0.1 convolution_convert_fusion.2
  66.7 0.7 copy.71
  67.4 3.2 %all-to-all-start.1 = ((bf16[4,2,2,3]{3,2,1,0:T(2,128)(2,1)}), bf16[4,2,2,3]{3,2,1,0:T(2,128)(2,1)S(1)}, u32[]{:S(2)}, u32[]{:S(2)}) async-start(bf16[4,2,2,3]{3,2,1,0:T(2,128)(2,1)} %bitcast.14), calls=%async_computation.1 | async-start | bytes 8192 | tf_op jit(solution)/shard_map/all_to_all | solution.py:80
  70.6 6.0 %copy.59 = bf16[4,2,3,3,16384]{4,1,3,2,0:T(2,128)(2,1)} copy(bf16[4,2,3,3,16384]{4,1,0,3,2:T(2,128)(2,1)} %reshape.90) | data formatting | bytes 4718592 | tf_op jit(solution)/shard_map/reshape | solution.py:77
  76.6 0.0 all-to-all-done.1
  76.6 3.8 %all-to-all-start = ((bf16[4,2,3,3,16384]{4,1,3,2,0:T(2,128)(2,1)}), bf16[4,2,3,3,16384]{4,1,3,2,0:T(2,128)(2,1)S(1)}, u32[]{:S(2)}, u32[]{:S(2)}) async-start(bf16[4,2,3,3,16384]{4,1,3,2,0:T(2,128)(2,1)} %copy.59), calls=%async_computation | async-start | bytes 4718592 | tf_op jit(solution)/shard_map/all_to_all | solution.py:79
  80.5 0.1 copy.73
  80.6 0.1 copy.65
  80.7 0.1 copy.72
  80.8 0.1 copy.63
  81.0 27.9 %all-to-all-done = bf16[4,2,3,3,16384]{4,1,3,2,0:T(2,128)(2,1)S(1)} async-done(((bf16[4,2,3,3,16384]{4,1,3,2,0:T(2,128)(2,1)}), bf16[4,2,3,3,16384]{4,1,3,2,0:T(2,128)(2,1)S(1)}, u32[]{:S(2)}, u32[]{:S(2)}) %all-to-all-start) | async-done | bytes 2359328 | tf_op jit(solution)/shard_map/all_to_all | solution.py:79
  108.9 2.4 %fusion.2 = bf16[4,2,3,3,16384]{4,1,3,2,0:T(2,128)(2,1)S(1)} fusion(bf16[4,2,3,3,16384]{4,1,3,2,0:T(2,128)(2,1)S(1)} %all-to-all-done, f32[4,2,3,3]{1,3,2,0:T(4,128)S(1)} %sqrt_multiply_fusion), kind=kLoop, calls=%fused_computation.7 | loop fusion | flops 3538944 | bytes 4718880 | tf_op jit(solution)/shard_map/convert_element_type | solution.py:35
  111.3 2.0 %copy.66 = bf16[4,2,3,3,16384]{4,1,0,3,2:T(2,128)(2,1)S(1)} copy(bf16[4,2,3,3,16384]{4,1,3,2,0:T(2,128)(2,1)S(1)} %fusion.2) | data formatting | bytes 4718592 | tf_op jit(solution)/shard_map/convert_element_type | solution.py:35
  113.4 2.4 %reshape.92 = bf16[8,3,3,16384]{3,0,2,1:T(8,128)(2,1)} reshape(bf16[4,2,3,3,16384]{4,1,0,3,2:T(2,128)(2,1)S(1)} %copy.66) | data formatting | bytes 4718592 | tf_op jit(solution)/shard_map/reshape | solution.py:82
  (6 shorter events, 0.1 us)
Async XLA Ops:
  6.5 50.9 %all-gather.2.cloned.1.call-start = ((), (), s32[]{:S(2)}) async-start(), calls=%async_computation.2 | async-start | bytes 1769472 | tf_op jit(solution)/shard_map/all_gather | solution.py:52
  67.4 9.2 %all-to-all-start.1 = ((bf16[4,2,2,3]{3,2,1,0:T(2,128)(2,1)}), bf16[4,2,2,3]{3,2,1,0:T(2,128)(2,1)S(1)}, u32[]{:S(2)}, u32[]{:S(2)}) async-start(bf16[4,2,2,3]{3,2,1,0:T(2,128)(2,1)} %bitcast.14), calls=%async_computation.1 | async-start | bytes 8192 | tf_op jit(solution)/shard_map/all_to_all | solution.py:80
  76.6 32.3 %all-to-all-start = ((bf16[4,2,3,3,16384]{4,1,3,2,0:T(2,128)(2,1)}), bf16[4,2,3,3,16384]{4,1,3,2,0:T(2,128)(2,1)S(1)}, u32[]{:S(2)}, u32[]{:S(2)}) async-start(bf16[4,2,3,3,16384]{4,1,3,2,0:T(2,128)(2,1)} %copy.59), calls=%async_computation | async-start | bytes 4718592 | tf_op jit(solution)/shard_map/all_to_all | solution.py:79
Sparse Core Ops, SparseCore 0:
  10.5 46.8 all-gather.1
where the time goes:
time: 123 us
  waiting for transfers between devices  70.1 us (57%)
  local copies, waits for them, and re-layouts  17.2 us (14%)
  between operations  13.5 us (11%)
  other arithmetic  9.97 us (8%)
  starting transfers between devices  6.98 us (6%)
  matrix products  4.84 us (4%)
    all_gather x1, waiting for transfers between devices, body(): piece = lax.all_gather(masked, 'dev', axis=0, tiled=True)  42.2 us
    all_to_all x1, waiting for transfers between devices, body(): lax.all_to_all(send_stack, 'grp', split_axis=0, concat_axis=0, tiled=True)  27.9 us
    reshape x2, local copies, waits for them, and re-layouts, body(): send_stack = send_stack.reshape((groups, CAP) + send_stack.shape[1:])  8.82 us
    dot_general x1, matrix products, body(): jnp.einsum('psr,rwf->pswf', select, piece, preferred_element_type=jnp.flo...  3.96 us
    all_to_all x1, starting transfers between devices, body(): lax.all_to_all(send_stack, 'grp', split_axis=0, concat_axis=0, tiled=True)  3.81 us
    all_to_all x1, starting transfers between devices, body(): lax.all_to_all(send_energy, 'grp', split_axis=0, concat_axis=0, tiled=True)  3.17 us
  transfers between devices with their start and end apart: 3, of which 2 were waited for; matrix products, arithmetic and copies ran while one was open for 9% of the time, Pallas kernels for 0%

commit v1 on v0

v1 whole, which is shorter than its diff:
```python
import functools

import jax
import jax.numpy as jnp
from jax import lax
from jax.experimental import pallas as pl
from jax.experimental.pallas import tpu as pltpu
from jax.sharding import PartitionSpec as P

CAP = 2
EPS = 1e-06
MAJOR = 4
CHUNKS = 4
LANES = 128


def kernel(groups, n_dev, windows, x_ref, part_ref, owner_ref, gain_ref, out_ref, *scratch):
    bufs = scratch[:CHUNKS]
    (send, part_in, own_in, acc_own, acc_part, inv_ref,
     zs, zr, xs, xr, os_, or_, ps, pr) = scratch[CHUNKS:]
    minor = n_dev // MAJOR
    per_dev = acc_own.shape[0]
    rows_out = groups * CAP
    height = gain_ref.shape[1]
    block_rows = x_ref.shape[1]
    slots = part_ref.shape[1]
    me_g = lax.axis_index("grp")
    me_d = lax.axis_index("dev")
    z = me_d // minor
    x = me_d % minor

    def other_group(delta):
        return lax.rem(me_g + delta, groups)

    def other_minor(delta):
        return z * minor + lax.rem(x + delta, minor)

    barrier = pltpu.get_barrier_semaphore()

    def greet(**where):
        pl.semaphore_signal(barrier, inc=1, device_id=where, device_id_type=pl.DeviceIdType.MESH)

    for delta in range(1, groups):
        greet(grp=other_group(delta))
    for delta in range(1, minor):
        greet(dev=other_minor(delta))

    @pl.when(z > 0)
    def _():
        greet(dev=me_d - minor)

    @pl.when(z < MAJOR - 1)
    def _():
        greet(dev=me_d + minor)

    for c in range(CHUNKS):
        bufs[c][me_d] = x_ref[c]
    own_in[me_g] = x_ref[...]
    acc_own[...] = jnp.zeros_like(acc_own)
    acc_part[...] = jnp.zeros_like(acc_part)

    owners = [owner_ref[p, 0] for p in range(slots)]
    partners = [part_ref[0, p] for p in range(slots)]
    dests = []
    for p in range(slots):
        rank = jnp.int32(0)
        for before in range(p):
            rank = rank + jnp.where(owners[before] == owners[p], 1, 0)
        dests.append(owners[p] * CAP + rank)
    chosen, filled = [], []
    for k in range(rows_out):
        index, used = jnp.int32(0), jnp.int32(0)
        for p in range(slots):
            index = jnp.where(dests[p] == k, partners[p], index)
            used = jnp.where(dests[p] == k, 1, used)
        chosen.append(index)
        filled.append(used)

    neighbours = jnp.where(z > 0, 1, 0) + jnp.where(z < MAJOR - 1, 1, 0)
    pl.semaphore_wait(barrier, groups - 1 + minor - 1 + neighbours)

    def remote(src, dst, send_sem, recv_sem, **where):
        return pltpu.make_async_remote_copy(
            src_ref=src, dst_ref=dst, send_sem=send_sem, recv_sem=recv_sem,
            device_id=where, device_id_type=pl.DeviceIdType.MESH)

    def own_copy(delta):
        return remote(x_ref, own_in.at[me_g], os_.at[delta - 1], or_.at[delta - 1],
                      grp=other_group(delta))

    def part_copy(delta, c):
        return remote(send.at[other_group(delta), c], part_in.at[me_g, c],
                      ps.at[delta - 1, c], pr.at[delta - 1, c], grp=other_group(delta))

    def chain_copy(up, dist, c, block):
        ref = bufs[c].at[block]
        way = 0 if up else 1
        target = me_d + minor if up else me_d - minor
        return remote(ref, ref, zs.at[way, dist, c], zr.at[way, dist, c], dev=target)

    def side_copy(number, delta, c, block):
        ref = bufs[c].at[block]
        return remote(ref, ref, xs.at[number, delta - 1, c], xr.at[number, delta - 1, c],
                      dev=other_minor(delta))

    def sources():
        yield None, 0, 0, None, me_d
        for dist in range(1, MAJOR):
            yield True, dist, dist, z >= dist, me_d - dist * minor
            yield False, dist, MAJOR - 1 + dist, z + dist < MAJOR, me_d + dist * minor

    def guarded(condition, run):
        if condition is None:
            run()
        else:
            pl.when(condition)(run)

    def each_send(way, dist, number, block, c, act):
        if dist + 1 < MAJOR:
            if way is None or way:
                guarded(z < MAJOR - 1, lambda: act(chain_copy(True, dist + 1, c, block)))
            if way is None or not way:
                guarded(z > 0, lambda: act(chain_copy(False, dist + 1, c, block)))
        for delta in range(1, minor):
            act(side_copy(number, delta, c, block))

    for delta in range(1, groups):
        own_copy(delta).start()

    def hop(at_dist, c):
        for way, dist, number, condition, block in sources():
            if dist != at_dist:
                continue

            def run(way=way, dist=dist, number=number, block=block):
                if dist:
                    chain_copy(way, dist, c, block).wait_recv()
                each_send(way, dist, number, block, c, lambda copy: copy.start())

            guarded(condition, run)

    def forward(c):
        for way, dist, number, condition, block in sources():
            def run(number=number, block=block):
                for delta in range(1, minor):
                    side_copy(number, delta, c, block).wait_recv()

            guarded(condition, run)
        for o in range(groups):
            for r in range(CAP):
                k = o * CAP + r
                taken = bufs[c][chosen[k]]
                taken = jnp.where(filled[k] > 0, taken, jnp.zeros_like(taken))
                send[o, c, pl.ds(r * block_rows, block_rows)] = taken
        for delta in range(1, groups):
            part_copy(delta, c).start()
        part_in[me_g, c] = send[me_g, c]

    def compute(c):
        if c == 0:
            for delta in range(1, groups):
                own_copy(delta).wait_recv()
        for delta in range(1, groups):
            part_copy(delta, c).wait_recv()
        gain = gain_ref[c]

        def one(row, carry):
            g = row // CAP
            r = row % CAP

            def piece(load, s, w, half):
                return load(((s * windows + w) * 2 + half) * height).astype(jnp.float32)

            def from_own(at):
                return own_in[g, c, pl.ds(at, height)]

            def from_part(at):
                base = pl.multiple_of(r * block_rows, block_rows)
                return part_in[g, c, pl.ds(base + at, height)]

            parts = [[[piece(from_part, s, w, h) for h in range(2)] for w in range(windows)]
                     for s in range(per_dev)]
            for s in range(per_dev):
                total = sum(v * v for pair in parts[s] for v in pair)
                acc_part[s, row] += total * gain
            for i in range(per_dev):
                own = [[piece(from_own, i, w, h) for h in range(2)] for w in range(windows)]
                total = sum(v * v for pair in own for v in pair)
                acc_own[i, row] += total * gain
                for j in range(per_dev):
                    real = sum(own[w][0] * parts[j][w][0] + own[w][1] * parts[j][w][1]
                               for w in range(windows))
                    imag = sum(own[w][1] * parts[j][w][0] - own[w][0] * parts[j][w][1]
                               for w in range(windows))
                    n = i * per_dev + j
                    out_ref[row, n, 0, c] = (real * gain).astype(jnp.bfloat16)
                    out_ref[row, n, 1, c] = (imag * gain).astype(jnp.bfloat16)
            return carry

        lax.fori_loop(0, rows_out, one, 0)

    for t in range(CHUNKS + MAJOR + 1):
        for dist in range(MAJOR):
            if 0 <= t - dist < CHUNKS:
                hop(dist, t - dist)
        if 0 <= t - MAJOR + 1 < CHUNKS:
            forward(t - MAJOR + 1)
        if 0 <= t - MAJOR - 1 < CHUNKS:
            compute(t - MAJOR - 1)

    entries = windows * 2 * CHUNKS * height * LANES

    def energy(acc, s):
        value = jnp.sum(jnp.sum(acc[s], axis=1), axis=-1, keepdims=True) / entries
        return value.astype(jnp.bfloat16).astype(jnp.float32) + EPS

    own_e = [energy(acc_own, s) for s in range(per_dev)]
    part_e = [energy(acc_part, s) for s in range(per_dev)]
    for i in range(per_dev):
        for j in range(per_dev):
            inverse = 1.0 / (windows * jnp.sqrt(own_e[i] * part_e[j]))
            inv_ref[i * per_dev + j] = jnp.broadcast_to(inverse, inv_ref.shape[1:])

    def scale(row, carry):
        for n in range(per_dev * per_dev):
            factor = inv_ref[n, pl.ds(row, 1)]
            for half in range(2):
                for c in range(CHUNKS):
                    stack = out_ref[row, n, half, c].astype(jnp.float32)
                    out_ref[row, n, half, c] = (stack * factor).astype(jnp.bfloat16)
        return carry

    lax.fori_loop(0, rows_out, scale, 0)

    for delta in range(1, groups):
        own_copy(delta).wait_send()
    for c in range(CHUNKS):
        for way, dist, number, condition, block in sources():
            def run(way=way, dist=dist, number=number, block=block):
                each_send(way, dist, number, block, c, lambda copy: copy.wait_send())

            guarded(condition, run)
        for delta in range(1, groups):
            part_copy(delta, c).wait_send()


def body(spectra, partners, owners, counts, gain):
    groups = lax.axis_size("grp")
    n_dev = lax.axis_size("dev")
    group = lax.axis_index("grp")
    device = lax.axis_index("dev")
    per_dev, windows, full = spectra.shape
    minor = n_dev // MAJOR
    height = full // 2 // CHUNKS // LANES
    group_count = jnp.sum(jnp.where(jnp.arange(groups) == group, counts, 0))
    station = device * per_dev + jnp.arange(per_dev, dtype=jnp.int32)
    live = (station < group_count).astype(jnp.bfloat16)
    masked = spectra * live[:, None, None]
    cut = masked.reshape(per_dev * windows * 2, CHUNKS, height, LANES).transpose(1, 0, 2, 3)
    block_rows = per_dev * windows * 2 * height
    cut = cut.reshape(CHUNKS, block_rows, LANES)
    rows = groups * CAP
    bf16, f32 = jnp.bfloat16, jnp.float32
    pairs = per_dev * per_dev
    dma = pltpu.SemaphoreType.DMA
    vmem = pl.BlockSpec(memory_space=pltpu.VMEM)
    smem = pl.BlockSpec(memory_space=pltpu.SMEM)
    out = pl.pallas_call(
        functools.partial(kernel, groups, n_dev, windows),
        out_shape=jax.ShapeDtypeStruct((rows, pairs, 2, CHUNKS, height, LANES), bf16),
        in_specs=[vmem, smem, smem, vmem],
        out_specs=vmem,
        scratch_shapes=[pltpu.VMEM((n_dev, block_rows, LANES), bf16)] * CHUNKS + [
            pltpu.VMEM((groups, CHUNKS, CAP * block_rows, LANES), bf16),
            pltpu.VMEM((groups, CHUNKS, CAP * block_rows, LANES), bf16),
            pltpu.VMEM((groups, CHUNKS, block_rows, LANES), bf16),
            pltpu.VMEM((per_dev, rows, height, LANES), f32),
            pltpu.VMEM((per_dev, rows, height, LANES), f32),
            pltpu.VMEM((pairs, rows, LANES), f32),
            dma((2, MAJOR, CHUNKS)),
            dma((2, MAJOR, CHUNKS)),
            dma((2 * MAJOR - 1, max(minor - 1, 1), CHUNKS)),
            dma((2 * MAJOR - 1, max(minor - 1, 1), CHUNKS)),
            dma((groups - 1,)),
            dma((groups - 1,)),
            dma((groups - 1, CHUNKS)),
            dma((groups - 1, CHUNKS)),
        ],
        compiler_params=pltpu.CompilerParams(
            collective_id=0, has_side_effects=True, vmem_limit_bytes=40 * 1024 * 1024),
    )(cut, partners, owners, gain.reshape(CHUNKS, height, LANES))
    return out.reshape(rows, per_dev, per_dev, full)


def solution(mesh):
    in_specs = (
        P(("grp", "dev"), None, None),
        P(("grp", "dev"), None),
        P(("grp", "dev"), None),
        P(),
        P(),
    )
    out_specs = P(("grp", "dev"), None, None, None)
    return jax.shard_map(body, mesh=mesh, in_specs=in_specs, out_specs=out_specs, check_vma=False)
```

time: 123 us -> 47.4 us (0.39)
  waiting for transfers between devices: 70.1 us -> 0 us
  Pallas kernels: 0 us -> 38.3 us
  between operations: 13.5 us -> 0.05 us
  local copies, waits for them, and re-layouts: 17.2 us -> 5.25 us
  starting transfers between devices: 6.98 us -> 0 us
  other arithmetic: 9.97 us -> 3.11 us
  matrix products: 4.84 us -> 0 us
    all_gather x1 -> x0, waiting for transfers between devices: 42.2 us -> none  [body(): piece = lax.all_gather(masked, 'dev', axis=0, tiled=True)]
    pallas_call x0 -> x1, Pallas kernels: none -> 38.3 us  [body(): pl.pallas_call(functools.partial(kernel, groups, n_dev, windows), out_sha...]
    all_to_all x2 -> x0, waiting for transfers between devices: 27.9 us -> none  [the longest x1 27.9 us: body(): lax.all_to_all(send_stack, 'grp', split_axis=0, concat_axis=0, tiled=True)]
    reshape x4 -> x3, local copies, waits for them, and re-layouts: 11.9 us -> 2.62 us  [the longest x1 2.45 us: body(): return out.reshape(rows, per_dev, per_dev, full)]
    all_to_all x2 -> x0, starting transfers between devices: 6.98 us -> none  [the longest x1 3.81 us: body(): lax.all_to_all(send_stack, 'grp', split_axis=0, concat_axis=0, tiled=True)]
    dot_general x3 -> x0, matrix products: 4.84 us -> none  [the longest x1 3.96 us: body(): jnp.einsum('psr,rwf->pswf', select, piece, preferred_element_type=jnp.flo...]
    convert_element_type x2 -> x0, other arithmetic: 4.32 us -> none  [the longest x1 2.43 us: normalize(): return (stack.astype(jnp.float32) / denom[..., None]).astype(jnp.bfloat16)]
    reduce_sum x2 -> x0, other arithmetic: 2.34 us -> none  [the longest x1 1.43 us: cross_spectra(): real_part = jnp.sum(a_own * a_part + b_own * b_part, axis=-2)]
  transfers between devices with their start and end apart: 3 -> 0, of which waited for: 2 -> 0; matrix products, arithmetic and copies ran while one was open for 9% -> 0% of each run, Pallas kernels for 0% -> 0%
where the time goes in v1:
time: 47.4 us; the launch traced here: 46.8 us
  Pallas kernels  38.3 us (81%)
  local copies, waits for them, and re-layouts  5.25 us (11%)
  other arithmetic  3.11 us (7%)
    pallas_call x1, Pallas kernels, body(): pl.pallas_call(functools.partial(kernel, groups, n_dev, windows), out_sha...  38.3 us
    reshape x1, local copies, waits for them, and re-layouts, body(): return out.reshape(rows, per_dev, per_dev, full)  2.45 us
    unnamed x5, local copies, waits for them, and re-layouts  2.14 us
    reduce_sum x1, other arithmetic, body(): group_count = jnp.sum(jnp.where(jnp.arange(groups) == group, counts, 0))  1.29 us
    mul x1, other arithmetic, body(): masked = spectra * live[:, None, None]  1.17 us

profile of v1, /device:TPU:0, one launch (start us, length us, event | category | flops | bytes accessed | tf_op | source)
XLA Modules:
  0.0 46.8 jit_solution(1321978694342453008)
XLA Ops:
  0.0 1.3 %fusion = s32[]{:T(128)} fusion(s32[4]{0:T(128)} %param.8, s32[]{:T(128)S(6)} %axis_index.25), kind=kLoop, calls=%fused_computation.3 | loop fusion | flops 11 | bytes 24 | tf_op jit(solution)/shard_map/reduce_sum | solution.py:255
  1.3 0.6 %compare_convert_fusion = bf16[3]{0:T(256)(128)(2,1)S(1)} fusion(s32[]{:T(128)} %fusion, s32[]{:T(128)S(6)} %mul.11), kind=kLoop, calls=%fused_computation.1 | loop fusion | flops 9 | bytes 14 | tf_op jit(solution)/shard_map/convert_element_type | solution.py:257
  1.9 0.7 %copy.10.owner_ref = s32[8,1]{1,0:T(8,128)S(1)} copy(s32[8,1]{0,1:T(1,128)} %param.7) | data formatting | bytes 64 | tf_op args[2]
  2.7 1.2 %broadcast_multiply_fusion = bf16[3,2,16384]{2,1,0:T(2,128)(2,1)S(1)} fusion(bf16[3,2,16384]{2,1,0:T(2,128)(2,1)} %param.5, bf16[3]{0:T(256)(128)(2,1)S(1)} %compare_convert_fusion), kind=kLoop, calls=%fused_computation | loop fusion | flops 98304 | bytes 393222 | tf_op jit(solution)/shard_map/mul | solution.py:258
  3.9 0.2 reshape.18
  4.0 0.0 copy-start
  4.1 0.7 %copy-done = f32[8192]{0:T(1024)S(1)} copy-done((f32[8192]{0:T(1024)S(1)}, f32[8192]{0:T(1024)}, u32[]{:S(2)}) %copy-start) | copy-done | bytes 32792
  4.8 0.0 copy-start.1
  4.8 0.7 %copy-done.1 = s32[1,8]{1,0:T(1,128)S(1)} copy-done((s32[1,8]{1,0:T(1,128)S(1)}, s32[1,8]{1,0:T(1,128)}, u32[]{:S(2)}) %copy-start.1) | copy-done | bytes 56
  5.5 38.3 %shard_map.55 = bf16[8,9,2,4,16,128]{5,4,3,2,1,0:T(8,128)(2,1)S(1)} custom-call(bf16[4,192,128]{2,1,0:T(8,128)(2,1)S(1)} %bitcast.8, s32[1,8]{1,0:T(1,128)S(1)} %copy-done.1, s32[8,1]{1,0:T(8,128)S(1)} %copy.10.owner_ref, f32[4,16,128]{2,1,0:T(8,128)S(1)} %bitcast.9), custom_call_target="tpu_custom_call" | custom-call | tf_op jit(solution)/shard_map/pallas_call | solution.py:268
  43.8 0.5 %copy.11 = bf16[8,9,2,4,16,128]{5,4,3,2,0,1:T(8,128)(2,1)S(1)} copy(bf16[8,9,2,4,16,128]{5,4,3,2,1,0:T(8,128)(2,1)S(1)} %shard_map.55) | data formatting | bytes 4718592 | tf_op jit(solution)/shard_map/pallas_call | solution.py:268
  44.3 2.4 %reshape.21 = bf16[8,3,3,16384]{3,0,2,1:T(8,128)(2,1)} reshape(bf16[8,9,2,4,16,128]{5,4,3,2,0,1:T(8,128)(2,1)S(1)} %copy.11) | data formatting | bytes 4718592 | tf_op jit(solution)/shard_map/reshape | solution.py:292
  (1 shorter events, 0.0 us)
Async XLA Ops:
  4.0 0.8 %copy-start = (f32[8192]{0:T(1024)S(1)}, f32[8192]{0:T(1024)}, u32[]{:S(2)}) copy-start(f32[8192]{0:T(1024)} %param.9) | copy-start | bytes 98308
  4.8 0.7 %copy-start.1 = (s32[1,8]{1,0:T(1,128)S(1)}, s32[1,8]{1,0:T(1,128)}, u32[]{:S(2)}) copy-start(s32[1,8]{1,0:T(1,128)} %part_ref.1) | copy-start | bytes 100
